TPU v7x, 128 devices: a whole 4x4x4 slice. The times are simulated.
128 devices in a mesh: row: 8 (over y, core), col: 16 (over z, x).
Axes of the slice: x: 4, y: 4, z: 4, core: 2. Of those that a mesh axis runs over, the one named last changes fastest.
Arguments:
- density: bfloat16 [64, 64, 64, 1024], P('row', 'col'), may hold values from -6 to 6
- bra_factor: bfloat16 [128, 2, 256, 1024], P(('row', 'col')), may hold values from -0.375 to 0.375
- ket_factor: bfloat16 [128, 2, 256, 1024], P(('row', 'col')), may hold values from -0.1875 to 0.1875
- bra_blocks: int32 [128, 2, 2], P(('row', 'col')), may hold values from 0 to 63, as said below
- ket_blocks: int32 [128, 2, 2], P(('row', 'col')), may hold values from 0 to 63, as said below
- block_slot: int32 [64], replicated, may hold values from 0 to 63, as said below
- task_list: int32 [128, 4], P(('row', 'col')), may hold values from 0 to 3, each once within a row
- task_count: int32 [128], P(('row', 'col')), may hold values from 3 to 4, as said below
Outputs:
- exchange: bfloat16 [64, 64, 64, 1024], P('row', 'col')
Inputs may be any that keep to these rules, and one draw needn't show every extreme that they name: `bra_blocks`: for each owner the 4 blocks of its bra pairs are stored in distinct device rows, where block x lies in device row block_slot[x] // 8. `ket_blocks`: for each owner the 4 blocks of its ket pairs are stored in distinct device columns, where block x lies in device column block_slot[x] // 4. `block_slot`: each number once. `task_list`: each row names every quartet index once. `task_count`: some owner has 4 live quartets.
All inputs are finite; a program needn't handle non-finite values.
Results may differ from a plain program's by a relative error of at most 0.0053.
Values may be sent and summed in bfloat16 or wider, within the bound.
No kernel may reach another device: no remote copies, remote signals or barrier semaphores. Data moves between devices by JAX's collectives and lax.ppermute only.
A program may use at most 192 MiB of HBM per device.

v0:
```python
import jax
import jax.numpy as jnp
from jax import lax
from jax.sharding import PartitionSpec as P

BS = 32


def lookup(table, index):
    hits = index[..., None] == jnp.arange(table.shape[0], dtype=jnp.int32)
    return jnp.sum(jnp.where(hits, table, 0), axis=-1)


def corner_plan(bra_rows, ket_rows, task_row, count, block_slot, shape_info):
    blk_row, blk_col, n_col = shape_info
    kets = ket_rows.shape[0]
    bra_which = task_row // kets
    ket_which = task_row % kets
    bra_store = lookup(block_slot, bra_rows)
    ket_store = lookup(block_slot, ket_rows)
    first = lookup(bra_store[:, 0], bra_which)
    second = lookup(bra_store[:, 1], bra_which)
    third = lookup(ket_store[:, 0], ket_which)
    fourth = lookup(ket_store[:, 1], ket_which)
    rows = jnp.stack([second, second, first, first], axis=1)
    columns = jnp.stack([fourth, third, fourth, third], axis=1)
    peers = rows // blk_row * n_col + columns // blk_col
    places = rows % blk_row * blk_col + columns % blk_col
    live = jnp.arange(task_row.shape[0], dtype=jnp.int32) < count
    return (peers, places, live, bra_which, ket_which)


def request_table(peers, places, live, devices):
    hits = (peers[..., None] == jnp.arange(devices, dtype=jnp.int32)) & live[:, None, None]
    wanted = jnp.any(hits, axis=(0, 1)).astype(jnp.int32)
    where_at = jnp.sum(jnp.where(hits, places[..., None], 0), axis=(0, 1))
    return jnp.stack([wanted, where_at], axis=1)


def shards(
    density, bra_factor, ket_factor, bra_blocks, ket_blocks, block_slot, task_list, task_count
):
    n_row = lax.axis_size("row")
    n_col = lax.axis_size("col")
    devices = n_row * n_col
    blk_row, blk_col, dens_count, block_area = density.shape
    side = BS
    local_blocks = blk_row * blk_col
    shape_info = (blk_row, blk_col, n_col)
    peers, places, live, bra_which, ket_which = corner_plan(
        bra_blocks[0], ket_blocks[0], task_list[0], task_count[0], block_slot, shape_info
    )
    outgoing = request_table(peers, places, live, devices)
    incoming = lax.all_to_all(outgoing, ("row", "col"), split_axis=0, concat_axis=0, tiled=True)
    flat = density.reshape(local_blocks, dens_count, block_area)
    chosen = jnp.take(flat, incoming[:, 1], axis=0)
    outgoing_blocks = jnp.where(incoming[:, 0, None, None] > 0, chosen, jnp.zeros_like(chosen))
    fetched = lax.all_to_all(
        outgoing_blocks, ("row", "col"), split_axis=0, concat_axis=0, tiled=True
    )

    def quartet(position, send):
        bra_one = lax.dynamic_index_in_dim(bra_factor[0], bra_which[position], 0, keepdims=False)
        ket_one = lax.dynamic_index_in_dim(ket_factor[0], ket_which[position], 0, keepdims=False)
        tile = lax.dot_general(
            bra_one, ket_one, (((0,), (0,)), ((), ())), preferred_element_type=jnp.float32
        )
        tile = tile.astype(jnp.bfloat16).reshape(side, side, side, side)
        corner_peers = peers[position]

        def grab(corner):
            picked = lax.dynamic_index_in_dim(fetched, corner_peers[corner], 0, keepdims=False)
            return picked.reshape(dens_count, side, side)

        updates = [
            jnp.einsum("ijkl,pik->pjl", tile, grab(3), preferred_element_type=jnp.float32),
            jnp.einsum("ijkl,pil->pjk", tile, grab(2), preferred_element_type=jnp.float32),
            jnp.einsum("ijkl,pjk->pil", tile, grab(1), preferred_element_type=jnp.float32),
            jnp.einsum("ijkl,pjl->pik", tile, grab(0), preferred_element_type=jnp.float32),
        ]
        for corner in range(4):
            rounded = updates[corner].reshape(dens_count, block_area).astype(jnp.bfloat16)
            send = lax.dynamic_update_index_in_dim(send, rounded, corner_peers[corner], 0)
        return send

    empty = jnp.zeros((devices, dens_count, block_area), jnp.bfloat16)
    send = lax.fori_loop(0, task_count[0], quartet, empty)
    received = lax.all_to_all(send, ("row", "col"), split_axis=0, concat_axis=0, tiled=True)
    placement_table = (incoming[:, 1, None] == jnp.arange(local_blocks, dtype=jnp.int32)) & (
        incoming[:, 0, None] > 0
    )
    placement_table = placement_table.astype(jnp.bfloat16)
    total = jnp.einsum("sn,spb->npb", placement_table, received, preferred_element_type=jnp.float32)
    return total.astype(jnp.bfloat16).reshape(blk_row, blk_col, dens_count, block_area)


def solution(mesh):
    in_specs = (
        P("row", "col", None, None),
        P(("row", "col"), None, None, None),
        P(("row", "col"), None, None, None),
        P(("row", "col"), None, None),
        P(("row", "col"), None, None),
        P(),
        P(("row", "col"), None),
        P(("row", "col")),
    )
    out_specs = P("row", "col", None, None)
    return jax.shard_map(shards, mesh=mesh, in_specs=in_specs, out_specs=out_specs, check_vma=False)
```

profile of v0, /device:TPU:1, one launch (start us, length us, event | category | flops | bytes accessed | tf_op | source)
XLA Modules:
  0.0 1034.2 jit_solution(3699548468185702499)
XLA Ops:
  0.7 0.9 fusion.35
  3.2 21.1 %all_to_all.22 = s32[128,1,2]{2,1,0:T(1,128)S(1)} all-to-all(s32[128,1,2]{2,1,0:T(1,128)S(1)} %copy.68), channel_id=1, replica_groups=mesh['row'=8,'col'=16] {'row','col'}, dimensions={0} | all-to-all | bytes 2048 | tf_op jit(solution)/shard_map/all_to_all | solution.py:54
  25.2 10.0 gather_fusion
  35.2 14.4 %select_select_fusion = bf16[128,64,1024]{2,1,0:T(8,128)(2,1)} fusion(bf16[128,64,1024]{2,1,0:T(8,128)(2,1)} %gather_fusion, pred[128]{0:T(512)(128)(4,1)S(1)} %get-tuple-element.111, pred[128]{0:T(512)(128)(4,1)S(1)} %get-tuple-element.110), kind=kLoop, calls=%fused_computation.30 | loop fusion | flops 16777216 | bytes 33554688 | tf_op jit(solution)/shard_map/jit(_where)/select_n | solution.py:57
  49.5 5.5 all-to-all-start.1
  55.1 234.0 %all-to-all-done.1 = bf16[128,64,1024]{2,1,0:T(8,128)(2,1)} async-done(((bf16[128,64,1024]{2,1,0:T(8,128)(2,1)}), bf16[128,64,1024]{2,1,0:T(8,128)(2,1)}, u32[]{:S(2)}, u32[]{:S(2)}) %all-to-all-start.1) | async-done | bytes 16777248 | tf_op jit(solution)/shard_map/all_to_all | solution.py:58
  289.0 30.0 %copy.70 = bf16[128,64,1024]{1,2,0:T(8,128)(2,1)} copy(bf16[128,64,1024]{2,1,0:T(8,128)(2,1)} %all-to-all-done.1) | data formatting | bytes 33554432 | tf_op jit(solution)/shard_map/while | solution.py:87
  319.1 6.0 broadcast.211
  325.0 470.6 %while.10 = (s32[]{:T(128)}, bf16[128,64,1024]{2,1,0:T(8,128)(2,1)}, s32[]{:T(128)}, s32[4,4]{1,0:T(4,128)S(1)}, bf16[128,64,1024]{1,2,0:T(8,128)(2,1)}, /*index...) while((s32[]{:T(128)}, ...), condition=%wide.region_9.10_spmd, body=%wide.region_8.9_spmd.sunk | while | flops 1075052544 | bytes 49283576 | solution.py:87
  347.1 1.9 convolution_convert_fusion.2
  349.1 7.8 reshape.573
  356.9 10.5 %copy.82 = bf16[32,32,32,32]{1,0,3,2:T(8,128)(2,1)} copy(bf16[32,32,32,32]{1,3,0,2:T(8,128)(2,1)} %bitcast.188) | data formatting | bytes 4194304 | tf_op jit(solution)/shard_map/while/body/ijkl,pik->pjl/dot_general | solution.py:76
  367.4 11.3 %dot_general.38 = bf16[1024,32,32]{0,2,1:T(8,128)(2,1)S(1)} reshape(bf16[32,32,32,32]{1,0,3,2:T(8,128)(2,1)} %copy.82) | data formatting | bytes 4194304 | tf_op jit(solution)/shard_map/while/body/ijkl,pik->pjl/dot_general | solution.py:76
  386.9 1.3 constant_dynamic-slice_fusion.8
  388.2 1.2 fusion.74
  389.3 6.7 fusion.75
  396.1 16.3 %copy.83 = bf16[32,32,32,32]{1,0,3,2:T(8,128)(2,1)} copy(bf16[32,32,32,32]{1,3,2,0:T(8,128)(2,1)} %bitcast.190) | data formatting | bytes 4194304 | tf_op jit(solution)/shard_map/while/body/ijkl,pjk->pil/dot_general | solution.py:78
  412.3 11.3 %dot_general.39 = bf16[1024,32,32]{0,2,1:T(8,128)(2,1)S(1)} reshape(bf16[32,32,32,32]{1,0,3,2:T(8,128)(2,1)} %copy.83) | data formatting | bytes 4194304 | tf_op jit(solution)/shard_map/while/body/ijkl,pjk->pil/dot_general | solution.py:78
  423.7 1.2 fusion.76
  424.8 15.3 %copy.84 = bf16[32,32,32,32]{1,0,3,2:T(8,128)(2,1)} copy(bf16[32,32,32,32]{3,1,2,0:T(8,128)(2,1)} %bitcast.191) | data formatting | bytes 4194304 | tf_op jit(solution)/shard_map/while/body/ijkl,pjl->pik/dot_general | solution.py:79
  440.2 11.3 %dot_general.40 = bf16[1024,32,32]{0,2,1:T(8,128)(2,1)S(1)} reshape(bf16[32,32,32,32]{1,0,3,2:T(8,128)(2,1)} %copy.84) | data formatting | bytes 4194304 | tf_op jit(solution)/shard_map/while/body/ijkl,pjl->pik/dot_general | solution.py:79
  451.5 1.2 fusion.77
  458.2 1.9 convolution_convert_fusion.2
  460.2 7.8 reshape.573
  468.0 10.5 %copy.82 = bf16[32,32,32,32]{1,0,3,2:T(8,128)(2,1)} copy(bf16[32,32,32,32]{1,3,0,2:T(8,128)(2,1)} %bitcast.188) | data formatting | bytes 4194304 | tf_op jit(solution)/shard_map/while/body/ijkl,pik->pjl/dot_general | solution.py:76
  478.5 11.3 %dot_general.38 = bf16[1024,32,32]{0,2,1:T(8,128)(2,1)S(1)} reshape(bf16[32,32,32,32]{1,0,3,2:T(8,128)(2,1)} %copy.82) | data formatting | bytes 4194304 | tf_op jit(solution)/shard_map/while/body/ijkl,pik->pjl/dot_general | solution.py:76
  498.0 1.3 constant_dynamic-slice_fusion.8
  499.2 1.2 fusion.74
  500.4 6.7 fusion.75
  507.1 16.3 %copy.83 = bf16[32,32,32,32]{1,0,3,2:T(8,128)(2,1)} copy(bf16[32,32,32,32]{1,3,2,0:T(8,128)(2,1)} %bitcast.190) | data formatting | bytes 4194304 | tf_op jit(solution)/shard_map/while/body/ijkl,pjk->pil/dot_general | solution.py:78
  523.4 11.3 %dot_general.39 = bf16[1024,32,32]{0,2,1:T(8,128)(2,1)S(1)} reshape(bf16[32,32,32,32]{1,0,3,2:T(8,128)(2,1)} %copy.83) | data formatting | bytes 4194304 | tf_op jit(solution)/shard_map/while/body/ijkl,pjk->pil/dot_general | solution.py:78
  534.7 1.2 fusion.76
  535.9 15.3 %copy.84 = bf16[32,32,32,32]{1,0,3,2:T(8,128)(2,1)} copy(bf16[32,32,32,32]{3,1,2,0:T(8,128)(2,1)} %bitcast.191) | data formatting | bytes 4194304 | tf_op jit(solution)/shard_map/while/body/ijkl,pjl->pik/dot_general | solution.py:79
  551.2 11.3 %dot_general.40 = bf16[1024,32,32]{0,2,1:T(8,128)(2,1)S(1)} reshape(bf16[32,32,32,32]{1,0,3,2:T(8,128)(2,1)} %copy.84) | data formatting | bytes 4194304 | tf_op jit(solution)/shard_map/while/body/ijkl,pjl->pik/dot_general | solution.py:79
  562.6 1.1 fusion.77
  569.2 1.9 convolution_convert_fusion.2
  571.2 7.8 reshape.573
  579.0 10.5 %copy.82 = bf16[32,32,32,32]{1,0,3,2:T(8,128)(2,1)} copy(bf16[32,32,32,32]{1,3,0,2:T(8,128)(2,1)} %bitcast.188) | data formatting | bytes 4194304 | tf_op jit(solution)/shard_map/while/body/ijkl,pik->pjl/dot_general | solution.py:76
  589.5 11.3 %dot_general.38 = bf16[1024,32,32]{0,2,1:T(8,128)(2,1)S(1)} reshape(bf16[32,32,32,32]{1,0,3,2:T(8,128)(2,1)} %copy.82) | data formatting | bytes 4194304 | tf_op jit(solution)/shard_map/while/body/ijkl,pik->pjl/dot_general | solution.py:76
  609.0 1.3 constant_dynamic-slice_fusion.8
  610.3 1.2 fusion.74
  611.4 6.7 fusion.75
  618.2 16.3 %copy.83 = bf16[32,32,32,32]{1,0,3,2:T(8,128)(2,1)} copy(bf16[32,32,32,32]{1,3,2,0:T(8,128)(2,1)} %bitcast.190) | data formatting | bytes 4194304 | tf_op jit(solution)/shard_map/while/body/ijkl,pjk->pil/dot_general | solution.py:78
  634.4 11.3 %dot_general.39 = bf16[1024,32,32]{0,2,1:T(8,128)(2,1)S(1)} reshape(bf16[32,32,32,32]{1,0,3,2:T(8,128)(2,1)} %copy.83) | data formatting | bytes 4194304 | tf_op jit(solution)/shard_map/while/body/ijkl,pjk->pil/dot_general | solution.py:78
  645.8 1.2 fusion.76
  646.9 15.3 %copy.84 = bf16[32,32,32,32]{1,0,3,2:T(8,128)(2,1)} copy(bf16[32,32,32,32]{3,1,2,0:T(8,128)(2,1)} %bitcast.191) | data formatting | bytes 4194304 | tf_op jit(solution)/shard_map/while/body/ijkl,pjl->pik/dot_general | solution.py:79
  662.3 11.3 %dot_general.40 = bf16[1024,32,32]{0,2,1:T(8,128)(2,1)S(1)} reshape(bf16[32,32,32,32]{1,0,3,2:T(8,128)(2,1)} %copy.84) | data formatting | bytes 4194304 | tf_op jit(solution)/shard_map/while/body/ijkl,pjl->pik/dot_general | solution.py:79
  673.6 1.2 fusion.77
  680.3 1.9 convolution_convert_fusion.2
  682.3 7.8 reshape.573
  690.1 10.5 %copy.82 = bf16[32,32,32,32]{1,0,3,2:T(8,128)(2,1)} copy(bf16[32,32,32,32]{1,3,0,2:T(8,128)(2,1)} %bitcast.188) | data formatting | bytes 4194304 | tf_op jit(solution)/shard_map/while/body/ijkl,pik->pjl/dot_general | solution.py:76
  700.6 11.3 %dot_general.38 = bf16[1024,32,32]{0,2,1:T(8,128)(2,1)S(1)} reshape(bf16[32,32,32,32]{1,0,3,2:T(8,128)(2,1)} %copy.82) | data formatting | bytes 4194304 | tf_op jit(solution)/shard_map/while/body/ijkl,pik->pjl/dot_general | solution.py:76
  720.1 1.3 constant_dynamic-slice_fusion.8
  721.3 1.2 fusion.74
  722.5 6.7 fusion.75
  729.2 16.3 %copy.83 = bf16[32,32,32,32]{1,0,3,2:T(8,128)(2,1)} copy(bf16[32,32,32,32]{1,3,2,0:T(8,128)(2,1)} %bitcast.190) | data formatting | bytes 4194304 | tf_op jit(solution)/shard_map/while/body/ijkl,pjk->pil/dot_general | solution.py:78
  745.5 11.3 %dot_general.39 = bf16[1024,32,32]{0,2,1:T(8,128)(2,1)S(1)} reshape(bf16[32,32,32,32]{1,0,3,2:T(8,128)(2,1)} %copy.83) | data formatting | bytes 4194304 | tf_op jit(solution)/shard_map/while/body/ijkl,pjk->pil/dot_general | solution.py:78
  756.8 1.1 fusion.76
  758.0 15.3 %copy.84 = bf16[32,32,32,32]{1,0,3,2:T(8,128)(2,1)} copy(bf16[32,32,32,32]{3,1,2,0:T(8,128)(2,1)} %bitcast.191) | data formatting | bytes 4194304 | tf_op jit(solution)/shard_map/while/body/ijkl,pjl->pik/dot_general | solution.py:79
  773.3 11.3 %dot_general.40 = bf16[1024,32,32]{0,2,1:T(8,128)(2,1)S(1)} reshape(bf16[32,32,32,32]{1,0,3,2:T(8,128)(2,1)} %copy.84) | data formatting | bytes 4194304 | tf_op jit(solution)/shard_map/while/body/ijkl,pjl->pik/dot_general | solution.py:79
  784.6 1.2 fusion.77
  795.6 209.4 %all_to_all.23 = bf16[128,64,1024]{2,1,0:T(8,128)(2,1)} all-to-all(bf16[128,64,1024]{2,1,0:T(8,128)(2,1)} %get-tuple-element.53), channel_id=1, replica_groups=mesh['row'=8,'col'=16] {'row','col'}, dimensions={0} | all-to-all | bytes 33554432 | tf_op jit(solution)/shard_map/all_to_all | solution.py:88
  1005.0 24.6 %fusion.19 = bf16[32,64,1024]{2,0,1:T(8,128)(2,1)S(1)} fusion(bf16[128,64,1024]{2,1,0:T(8,128)(2,1)} %all_to_all.23, s32[128]{0:T(128)S(1)} %copy-done.2, pred[128]{0:T(512)(128)(4,1)S(1)} %copy-done.1), kind=kOutput, calls=%fused_computation.31 | convolution fusion | flops 538976256 | bytes 20972160 | tf_op jit(solution)/shard_map/sn,spb->npb/dot_general | solution.py:93
  1029.6 4.3 copy.74
  (38 shorter events, 10.1 us)
Async XLA Ops:
  25.2 10.0 copy-start
  49.5 239.5 %all-to-all-start.1 = ((bf16[128,64,1024]{2,1,0:T(8,128)(2,1)}), bf16[128,64,1024]{2,1,0:T(8,128)(2,1)}, u32[]{:S(2)}, u32[]{:S(2)}) async-start(bf16[128,64,1024]{2,1,0:T(8,128)(2,1)} %select_select_fusion), calls=%async_computation.1 | async-start | bytes 33554432 | tf_op jit(solution)/shard_map/all_to_all | solution.py:58
  795.6 209.4 %copy-start.1 = (pred[128]{0:T(512)(128)(4,1)S(1)}, pred[128]{0:T(512)(128)(4,1)}, u32[]{:S(2)}) copy-start(pred[128]{0:T(512)(128)(4,1)} %copy-done) | copy-start | bytes 388
  795.6 209.4 %copy-start.2 = (s32[128]{0:T(128)S(1)}, s32[128]{0:T(128)}, u32[]{:S(2)}) copy-start(s32[128]{0:T(128)} %get-tuple-element.108) | copy-start | bytes 1540
where the time goes:
time: 1040 us; the launch traced here: 1030 us
  local copies, waits for them, and re-layouts  399 us (38%)
  waiting for transfers between devices  234 us (22%)
  blocking collectives  230 us (22%)
  loops' own time  73.6 us (7%)
  matrix products  73.2 us (7%)
  other arithmetic  17.2 us (2%)
    all_to_all x1, waiting for transfers between devices, shards(): lax.all_to_all(outgoing_blocks, ('row', 'col'), split_axis=0, concat_axis...  234 us
    all_to_all x1, blocking collectives, shards(): lax.all_to_all(send, ('row', 'col'), split_axis=0, concat_axis=0, tiled=T...  209 us
    dot_general x8, local copies, waits for them, and re-layouts, quartet(): jnp.einsum('ijkl,pjk->pil', tile, grab(1), preferred_element_type=jnp.flo...  110 us
    dot_general x8, local copies, waits for them, and re-layouts, quartet(): jnp.einsum('ijkl,pjl->pik', tile, grab(0), preferred_element_type=jnp.flo...  107 us
    dot_general x8, local copies, waits for them, and re-layouts, quartet(): jnp.einsum('ijkl,pik->pjl', tile, grab(3), preferred_element_type=jnp.flo...  87.3 us
    another operation x1, loops' own time, shards(): send = lax.fori_loop(0, task_count[0], quartet, empty)  73.6 us
    reshape x4, local copies, waits for them, and re-layouts, quartet(): tile = tile.astype(jnp.bfloat16).reshape(side, side, side, side)  31.4 us
    while x1, local copies, waits for them, and re-layouts, shards(): send = lax.fori_loop(0, task_count[0], quartet, empty)  30 us
  transfers between devices with their start and end apart: 1, of which 1 were waited for; matrix products, arithmetic and copies ran while one was open for 0% of the time, Pallas kernels for 0%

commit v1 on v0

v1 whole, which is shorter than its diff:
```python
import functools

import jax
import jax.numpy as jnp
from jax import lax
from jax.experimental import pallas as pl
from jax.experimental.pallas import tpu as pltpu
from jax.sharding import PartitionSpec as P

SIDE = 32
AREA = SIDE * SIDE
LANES = 128
GROUP = LANES // SIDE
BF16 = jnp.bfloat16
F32 = jnp.float32
AXES = ("row", "col")


def swap_matrix():
    rows = lax.broadcasted_iota(jnp.int32, (AREA, AREA), 0)
    columns = lax.broadcasted_iota(jnp.int32, (AREA, AREA), 1)
    hit = columns == (rows % SIDE) * SIDE + rows // SIDE
    return jnp.where(hit, 1.0, 0.0).astype(BF16)


def mm(a, b, dims):
    return lax.dot_general(a, b, (dims, ((), ())), preferred_element_type=F32)


NN = ((1,), (0,))
NT = ((1,), (1,))


def tiles_kernel(live_ref, bra_ref, ket_ref, out_ref, swap_ref, bra_nat, bra_swap, g_ref):
    step = pl.program_id(0)

    @pl.when(step == 0)
    def _():
        swap_ref[...] = swap_matrix()

    @pl.when(step % 2 == 0)
    def _():
        bra = bra_ref[0]
        bra_nat[...] = bra.astype(F32).T.astype(BF16)
        bra_swap[...] = mm(swap_ref[...], bra, NT).astype(BF16)

    lane = lax.broadcasted_iota(jnp.int32, (SIDE, LANES), 1)
    low_half = lane < LANES // 2
    low_part = lane % (LANES // 2) < SIDE

    def build(source_ref, which):
        def chunk(high, carry):
            rows = source_ref[pl.ds(pl.multiple_of(high * LANES, LANES), LANES), :]
            g_ref[...] = mm(rows, ket_ref[0], NN)
            out_at = pl.ds(pl.multiple_of(high * LANES, LANES), LANES)
            for kh in range(AREA // LANES):
                at = pl.ds(kh * LANES, LANES)
                a = [g_ref[pl.ds(n * SIDE, SIDE), at] for n in range(GROUP)]
                b0 = jnp.where(low_half, a[0], pltpu.roll(a[2], 64, 1))
                b2 = jnp.where(low_half, pltpu.roll(a[0], 64, 1), a[2])
                b1 = jnp.where(low_half, a[1], pltpu.roll(a[3], 64, 1))
                b3 = jnp.where(low_half, pltpu.roll(a[1], 64, 1), a[3])
                c = [
                    jnp.where(low_part, b0, pltpu.roll(b1, 32, 1)),
                    jnp.where(low_part, pltpu.roll(b0, 96, 1), b1),
                    jnp.where(low_part, b2, pltpu.roll(b3, 32, 1)),
                    jnp.where(low_part, pltpu.roll(b2, 96, 1), b3),
                ]
                for n in range(GROUP):
                    row = (kh * GROUP + n) * SIDE
                    out_ref[0, which, pl.ds(row, SIDE), out_at] = c[n].astype(BF16)
            return carry

        lax.fori_loop(0, AREA // LANES, chunk, 0)

    @pl.when(live_ref[step] > 0)
    def _():
        build(bra_swap, 0)
        build(bra_nat, 1)


def tiles_call(live, bra, ket):
    rank = bra.shape[1]
    return pl.pallas_call(
        tiles_kernel,
        out_shape=jax.ShapeDtypeStruct((4, 2, AREA, AREA), BF16),
        grid=(4,),
        in_specs=[
            pl.BlockSpec(memory_space=pltpu.SMEM),
            pl.BlockSpec((1, rank, AREA), lambda t: (t // 2, 0, 0)),
            pl.BlockSpec((1, rank, AREA), lambda t: (t % 2, 0, 0)),
        ],
        out_specs=pl.BlockSpec((1, 2, AREA, AREA), lambda t: (t, 0, 0, 0)),
        scratch_shapes=[
            pltpu.VMEM((AREA, AREA), BF16),
            pltpu.VMEM((AREA, rank), BF16),
            pltpu.VMEM((AREA, rank), BF16),
            pltpu.VMEM((LANES, AREA), F32),
        ],
        compiler_params=pltpu.CompilerParams(vmem_limit_bytes=48 * 1024 * 1024),
        cost_estimate=pl.CostEstimate(flops=6_000_000_000, bytes_accessed=20_000_000, transcendentals=0),
    )(live, bra, ket)


def contract_kernel(live_ref, tile_ref, d_ref, out_ref, swap_ref):
    step = pl.program_id(0)
    dens = d_ref.shape[2]

    @pl.when(step == 0)
    def _():
        swap_ref[...] = swap_matrix()

    @pl.when(live_ref[step] > 0)
    def _():
        swap = swap_ref[...]
        d_ac = mm(d_ref[0, 0], swap, NN).astype(BF16)
        d_bc = mm(d_ref[1, 0], swap, NN).astype(BF16)
        t_one = tile_ref[0, 0]
        t_two = tile_ref[0, 1]
        out_ref[1, 1] = mm(d_ac, t_one, NN).astype(BF16)
        up_ac = mm(d_ref[1, 1], t_one, NT).astype(BF16)
        out_ref[0, 1] = mm(d_bc, t_two, NN).astype(BF16)
        up_bc = mm(d_ref[0, 1], t_two, NT).astype(BF16)
        out_ref[0, 0] = mm(up_ac, swap, NN).astype(BF16)
        out_ref[1, 0] = mm(up_bc, swap, NN).astype(BF16)

    @pl.when(live_ref[step] == 0)
    def _():
        out_ref[...] = jnp.zeros_like(out_ref)


def contract_call(live, tiles, blocks):
    dens = blocks.shape[2]
    return pl.pallas_call(
        contract_kernel,
        out_shape=jax.ShapeDtypeStruct(blocks.shape, BF16),
        grid=(4,),
        in_specs=[
            pl.BlockSpec(memory_space=pltpu.SMEM),
            pl.BlockSpec((1, 2, AREA, AREA), lambda t: (t, 0, 0, 0)),
            pl.BlockSpec((2, 2, dens, AREA), lambda t: (t // 2, t % 2, 0, 0)),
        ],
        out_specs=pl.BlockSpec((2, 2, dens, AREA), lambda t: (t // 2, t % 2, 0, 0)),
        scratch_shapes=[pltpu.VMEM((AREA, AREA), BF16)],
        compiler_params=pltpu.CompilerParams(vmem_limit_bytes=48 * 1024 * 1024),
        cost_estimate=pl.CostEstimate(flops=6_000_000_000, bytes_accessed=20_000_000, transcendentals=0),
    )(live, tiles, blocks)


def split_parts(blocks):
    n, dens, area = blocks.shape
    x = blocks.reshape(n, dens // 8, 2, 4, area // LANES, LANES)
    x = x.transpose(1, 4, 2, 0, 3, 5)
    return x.reshape(dens * area // 512, n, 4, LANES)


def join_parts(parts, dens, area):
    _, n, _, _ = parts.shape
    x = parts.reshape(dens // 8, area // LANES, 2, n, 4, LANES)
    x = x.transpose(3, 0, 2, 4, 1, 5)
    return x.reshape(n, dens, area)


def exchange_all(x):
    return lax.all_to_all(x, AXES, split_axis=0, concat_axis=0, tiled=True)


def shards(density, bra_factor, ket_factor, bra_blocks, ket_blocks, block_slot, task_list, task_count):
    n_col = lax.axis_size("col")
    devices = lax.axis_size("row") * n_col
    blk_row, blk_col, dens, area = density.shape
    local = blk_row * blk_col

    names = jnp.concatenate([bra_blocks[0].reshape(4), ket_blocks[0].reshape(4)])
    hits = names[:, None] == jnp.arange(block_slot.shape[0], dtype=jnp.int32)
    slots = jnp.sum(jnp.where(hits, block_slot[None, :], 0), axis=-1)
    listed = jnp.arange(4, dtype=jnp.int32) < task_count[0]
    live = jnp.any(
        (task_list[0][None, :] == jnp.arange(4, dtype=jnp.int32)[:, None]) & listed[None, :], axis=1
    ).astype(jnp.int32)

    row = jnp.zeros((4, LANES), BF16).at[0, :8].set(slots.astype(BF16))
    row = jnp.broadcast_to(row[None, None], (devices, 1, 4, LANES))
    outgoing = jnp.concatenate([split_parts(density.reshape(local, dens, area)), row], axis=1)
    arrived = exchange_all(outgoing)
    table = arrived[:, local, 0, :8].astype(F32).astype(jnp.int32)
    xs, ys = table[:, :4, None], table[:, None, 4:]
    place = ((xs // blk_row) * n_col + ys // blk_col, (xs % blk_row) * blk_col + ys % blk_col)
    fetch_at = (place[0] * (local + 1) + place[1]).reshape(devices * 16)
    store_at = (place[0] * local + place[1]).reshape(devices * 16)
    picked = jnp.take(arrived.reshape(devices * (local + 1), 4, LANES), fetch_at, axis=0)
    fetched = exchange_all(picked.reshape(devices, 16, 4, LANES))
    corners = join_parts(fetched, dens, area).reshape(4, 4, dens, area)

    tiles = tiles_call(live, bra_factor[0], ket_factor[0])
    updates = contract_call(live, tiles, corners)

    returned = exchange_all(split_parts(updates.reshape(16, dens, area)))
    hot = (jnp.arange(devices * local, dtype=jnp.int32)[:, None] == store_at[None, :]).astype(BF16)
    total = lax.dot_general(
        hot, returned.reshape(devices * 16, 512), (((1,), (0,)), ((), ())), preferred_element_type=F32
    )
    total = total.astype(BF16).reshape(devices, local, 4, LANES)
    final = join_parts(exchange_all(total), dens, area)
    return final.reshape(blk_row, blk_col, dens, area)


def solution(mesh):
    in_specs = (
        P("row", "col", None, None),
        P(AXES, None, None, None),
        P(AXES, None, None, None),
        P(AXES, None, None),
        P(AXES, None, None),
        P(),
        P(AXES, None),
        P(AXES),
    )
    out_specs = P("row", "col", None, None)
    return jax.shard_map(shards, mesh=mesh, in_specs=in_specs, out_specs=out_specs, check_vma=False)
```

time: 1040 us -> 295 us (0.28)
  local copies, waits for them, and re-layouts: 399 us -> 65.4 us
  waiting for transfers between devices: 234 us -> 33.9 us
  blocking collectives: 230 us -> 123 us
  loops' own time: 73.6 us -> 0 us
  matrix products: 73.2 us -> 10.4 us
  Pallas kernels: 0 us -> 38.2 us
  other arithmetic: 17.2 us -> 3.51 us
  starting transfers between devices: 5.53 us -> 19.1 us
    dot_general x24 -> x0, local copies, waits for them, and re-layouts: 304 us -> none  [the longest x8 110 us: quartet(): jnp.einsum('ijkl,pjk->pil', tile, grab(1), preferred_element_type=jnp.flo...]
    all_to_all x1 -> x2, waiting for transfers between devices: 234 us -> 33.9 us  [exchange_all(): return lax.all_to_all(x, AXES, split_axis=0, concat_axis=0, tiled=True)]
    all_to_all x2, blocking collectives: 230 us -> 123 us  [exchange_all(): return lax.all_to_all(x, AXES, split_axis=0, concat_axis=0, tiled=True)]
    another operation x1 -> x0, loops' own time: 73.6 us -> none  [shards(): send = lax.fori_loop(0, task_count[0], quartet, empty)]
    dot_general x21 -> x1, matrix products: 73.2 us -> 10.4 us  [shards(): lax.dot_general(hot, returned.reshape(devices * 16, 512), (((1,), (0,)),...]
    pallas_call x0 -> x2, Pallas kernels: none -> 38.2 us  [the longest x1 23.6 us: tiles_call(): pl.pallas_call(tiles_kernel, out_shape=jax.ShapeDtypeStruct((4, 2, AREA,...]
    while x1 -> x0, local copies, waits for them, and re-layouts: 30 us -> none  [shards(): send = lax.fori_loop(0, task_count[0], quartet, empty)]
    reshape x5 -> x2, local copies, waits for them, and re-layouts: 35.7 us -> 13.7 us  [the longest x1 6.9 us: shards(): total = total.astype(BF16).reshape(devices, local, 4, LANES)]
  transfers between devices with their start and end apart: 1 -> 2, of which waited for: 1 -> 2; matrix products, arithmetic and copies ran while one was open for 0% -> 0% of each run, Pallas kernels for 0% -> 8%
where the time goes in v1:
time: 295 us; the launch traced here: 294 us
  blocking collectives  123 us (42%)
  local copies, waits for them, and re-layouts  65.4 us (22%)
  Pallas kernels  38.2 us (13%)
  waiting for transfers between devices  33.9 us (11%)
  starting transfers between devices  19.1 us (6%)
  matrix products  10.4 us (4%)
  other arithmetic  3.51 us (1%)
    all_to_all x2, blocking collectives, exchange_all(): return lax.all_to_all(x, AXES, split_axis=0, concat_axis=0, tiled=True)  123 us
    all_to_all x2, waiting for transfers between devices, exchange_all(): return lax.all_to_all(x, AXES, split_axis=0, concat_axis=0, tiled=True)  33.9 us
    pallas_call x1, Pallas kernels, tiles_call(): pl.pallas_call(tiles_kernel, out_shape=jax.ShapeDtypeStruct((4, 2, AREA,...  23.6 us
    all_to_all x2, starting transfers between devices, exchange_all(): return lax.all_to_all(x, AXES, split_axis=0, concat_axis=0, tiled=True)  19.1 us
    gather x2, local copies, waits for them, and re-layouts, shards(): jnp.take(arrived.reshape(devices * (local + 1), 4, LANES), fetch_at, axis=0)  18.7 us
    pallas_call x1, Pallas kernels, contract_call(): pl.pallas_call(contract_kernel, out_shape=jax.ShapeDtypeStruct(blocks.sha...  14.6 us
    dot_general x1, matrix products, shards(): lax.dot_general(hot, returned.reshape(devices * 16, 512), (((1,), (0,)),...  10.4 us
    another operation x1, local copies, waits for them, and re-layouts, shards(): return final.reshape(blk_row, blk_col, dens, area)  7.27 us
  transfers between devices with their start and end apart: 2, of which 2 were waited for; matrix products, arithmetic and copies ran while one was open for 0% of the time, Pallas kernels for 8%

profile of v1, /device:TPU:1, one launch (start us, length us, event | category | flops | bytes accessed | tf_op | source)
XLA Modules:
  0.0 294.4 jit_solution(9835641382287324620)
XLA Ops:
  0.0 0.8 reshape_squeeze.6
  0.8 0.8 reshape_squeeze.7
  1.5 0.1 pad_add_fusion
  1.6 0.8 select_reduce_fusion
  2.4 3.3 %copy.45 = bf16[256,8,8,128]{3,2,1,0:T(8,128)(2,1)S(1)} copy(bf16[256,8,8,128]{3,1,2,0:T(8,128)(2,1)} %bitcast.55) | data formatting | bytes 8388608
  5.7 2.7 copy.35
  8.5 0.1 broadcast_in_dim.26
  8.6 1.2 pad_maximum_fusion
  9.8 1.7 copy.36
  11.6 66.3 %all_to_all.20 = bf16[128,33,4,128]{3,2,1,0:T(4,128)(2,1)S(1)} all-to-all(bf16[128,33,4,128]{3,2,1,0:T(4,128)(2,1)S(1)} %copy.36), channel_id=1, replica_groups=mesh['row'=8,'col'=16] {'row','col'}, dimensions={0} | all-to-all | bytes 8650752 | tf_op jit(solution)/shard_map/all_to_all | solution.py:165
  77.9 0.0 copy-start.2
  77.9 2.0 copy-done.2
  79.9 0.1 fusion.7
  80.0 0.1 fusion.5
  80.1 0.1 fusion.6
  80.2 0.4 add_add_fusion
  80.7 0.3 add.150
  80.9 0.1 copy.37
  81.1 16.8 %gather_fusion = bf16[2048,4,128]{2,1,0:T(4,128)(2,1)} fusion(bf16[4224,4,128]{2,1,0:T(4,128)(2,1)} %bitcast.51, s32[2048]{0:T(1024)S(1)} %broadcast_clamp_fusion), kind=kCustom, calls=%fused_computation | custom fusion | bytes 4202496 | tf_op jit(solution)/shard_map/jit(_take)/gather | solution.py:191
  97.9 1.9 copy.39
  99.8 0.1 copy.38
  99.9 0.5 broadcast_select_fusion
  100.3 0.0 copy-start.3
  100.4 0.0 copy-start
  100.4 0.0 copy-start.1
  100.4 2.0 copy.40
  102.4 5.0 %all-to-all-start.1 = ((bf16[128,16,4,128]{3,1,2,0:T(8,128)(2,1)}), bf16[128,16,4,128]{3,1,2,0:T(8,128)(2,1)}, u32[]{:S(2)}, u32[]{:S(2)}) async-start(bf16[128,16,4,128]{3,1,2,0:T(8,128)(2,1)} %copy.40), calls=%async_computation.1 | async-start | bytes 4194304 | tf_op jit(solution)/shard_map/all_to_all | solution.py:165
  108.0 0.0 copy-done.3
  108.0 0.1 fusion.13
  108.1 0.0 copy-done
  108.1 0.0 copy-done.1
  108.1 23.6 %shard_map.82.tile_ref = bf16[4,2,1024,1024]{3,2,1,0:T(8,128)(2,1)} custom-call(s32[4]{0:T(128)S(1)} %convert_element_type.33.live_ref, bf16[2,256,1024]{2,1,0:T(8,128)(2,1)S(1)} %bitcast.45, bf16[2,256,1024]{2,1,0:T(8,128)(2,1)S(1)} %bitcast.46), custom_call_target="tpu_custom_call" | custom-call | flops 6000000000 | bytes 20000000 | tf_op jit(solution)/shard_map/pallas_call | solution.py:84
  131.8 4.7 %all-to-all-done.1 = bf16[128,16,4,128]{3,1,2,0:T(8,128)(2,1)} async-done(((bf16[128,16,4,128]{3,1,2,0:T(8,128)(2,1)}), bf16[128,16,4,128]{3,1,2,0:T(8,128)(2,1)}, u32[]{:S(2)}, u32[]{:S(2)}) %all-to-all-start.1) | async-done | bytes 2097184 | tf_op jit(solution)/shard_map/all_to_all | solution.py:165
  136.5 4.3 %copy.41 = bf16[16,8,2,4,8,128]{5,4,3,2,1,0:T(8,128)(2,1)} copy(bf16[16,8,2,4,8,128]{5,0,3,2,4,1:T(8,128)(2,1)} %bitcast.13) | data formatting | bytes 4194304 | tf_op jit(solution)/shard_map/transpose | solution.py:160
  140.8 2.8 reshape_reshape.13.d_ref
  143.6 14.6 %shard_map.83 = bf16[4,4,64,1024]{3,2,1,0:T(8,128)(2,1)S(1)} custom-call(s32[4]{0:T(128)S(1)} %convert_element_type.33.live_ref, bf16[4,2,1024,1024]{3,2,1,0:T(8,128)(2,1)} %shard_map.82.tile_ref, bf16[4,4,64,1024]{3,2,1,0:T(8,128)(2,1)S(1)} %reshape_reshape.13.d_ref), custom_call_target="tpu_custom_call" | custom-call | flops 6000000000 | bytes 20000000 | tf_op jit(solution)/shard_map/pallas_call | solution.py:134
  158.2 0.6 copy.46
  158.8 2.8 copy.42
  161.6 14.1 %all-to-all-start.2 = ((bf16[128,16,4,128]{3,1,2,0:T(8,128)(2,1)}), bf16[128,16,4,128]{3,1,2,0:T(8,128)(2,1)S(1)}, u32[]{:S(2)}, u32[]{:S(2)}) async-start(bf16[128,16,4,128]{3,1,2,0:T(8,128)(2,1)} %bitcast.52), calls=%async_computation.2 | async-start | bytes 4194304 | tf_op jit(solution)/shard_map/all_to_all | solution.py:165
  175.7 0.3 add.145
  176.0 29.2 %all-to-all-done.2 = bf16[128,16,4,128]{3,1,2,0:T(8,128)(2,1)S(1)} async-done(((bf16[128,16,4,128]{3,1,2,0:T(8,128)(2,1)}), bf16[128,16,4,128]{3,1,2,0:T(8,128)(2,1)S(1)}, u32[]{:S(2)}, u32[]{:S(2)}) %all-to-all-start.2) | async-done | bytes 2097184 | tf_op jit(solution)/shard_map/all_to_all | solution.py:165
  205.1 1.2 copy.43
  206.3 10.4 %fusion.2 = bf16[4096,512]{1,0:T(8,128)(2,1)} fusion(s32[2048]{0:T(1024)S(1)} %add.145, bf16[256,8,4,128]{3,2,1,0:T(4,128)(2,1)S(1)} %bitcast.56), kind=kOutput, calls=%fused_computation.4 | convolution fusion | flops 8600420352 | bytes 6299648 | tf_op jit(solution)/shard_map/dot_general | solution.py:200
  216.7 6.9 %reshape.248 = bf16[128,32,4,128]{3,2,1,0:T(4,128)(2,1)} reshape(bf16[4096,512]{1,0:T(8,128)(2,1)} %fusion.2) | data formatting | bytes 8388608 | tf_op jit(solution)/shard_map/reshape | solution.py:203
  223.6 56.8 %all_to_all.21 = bf16[128,32,4,128]{3,2,1,0:T(4,128)(2,1)S(1)} all-to-all(bf16[128,32,4,128]{3,2,1,0:T(4,128)(2,1)} %reshape.248), channel_id=1, replica_groups=mesh['row'=8,'col'=16] {'row','col'}, dimensions={0} | all-to-all | bytes 8388608 | tf_op jit(solution)/shard_map/all_to_all | solution.py:165
  280.3 6.8 %copy.53 = bf16[8,8,2,32,4,128]{5,1,4,2,0,3:T(8,128)(2,1)} copy(bf16[8,8,2,32,4,128]{5,4,3,2,1,0:T(4,128)(2,1)S(1)} %bitcast.48) | data formatting | bytes 8388608 | tf_op jit(solution)/shard_map/reshape | solution.py:159
  287.1 7.3 %reshape_reshape.15 = bf16[8,4,64,1024]{3,2,1,0:T(8,128)(2,1)} reshape(bf16[32,8,2,4,8,128]{5,4,3,2,1,0:T(8,128)(2,1)} %bitcast.49) | data formatting | bytes 8388608 | tf_op jit(solution)/shard_map/reshape;reshape | solution.py:205
  (7 shorter events, 0.1 us)
Async XLA Ops:
  77.9 2.0 copy-start.2
  100.3 7.7 %copy-start.3 = (s32[1,4]{1,0:T(1,128)S(1)}, s32[1,4]{1,0:T(1,128)}, u32[]{:S(2)}) copy-start(s32[1,4]{1,0:T(1,128)} %param.16) | copy-start | bytes 52
  100.4 7.8 %copy-start = (bf16[1,2,256,1024]{3,2,1,0:T(8,128)(2,1)S(1)}, bf16[1,2,256,1024]{3,2,1,0:T(8,128)(2,1)}, u32[]{:S(2)}) copy-start(bf16[1,2,256,1024]{3,2,1,0:T(8,128)(2,1)} %param.11) | copy-start | bytes 3145732
  100.4 7.8 %copy-start.1 = (bf16[1,2,256,1024]{3,2,1,0:T(8,128)(2,1)S(1)}, bf16[1,2,256,1024]{3,2,1,0:T(8,128)(2,1)}, u32[]{:S(2)}) copy-start(bf16[1,2,256,1024]{3,2,1,0:T(8,128)(2,1)} %param.12) | copy-start | bytes 3145732
  102.4 34.2 %all-to-all-start.1 = ((bf16[128,16,4,128]{3,1,2,0:T(8,128)(2,1)}), bf16[128,16,4,128]{3,1,2,0:T(8,128)(2,1)}, u32[]{:S(2)}, u32[]{:S(2)}) async-start(bf16[128,16,4,128]{3,1,2,0:T(8,128)(2,1)} %copy.40), calls=%async_computation.1 | async-start | bytes 4194304 | tf_op jit(solution)/shard_map/all_to_all | solution.py:165
  161.6 43.5 %all-to-all-start.2 = ((bf16[128,16,4,128]{3,1,2,0:T(8,128)(2,1)}), bf16[128,16,4,128]{3,1,2,0:T(8,128)(2,1)S(1)}, u32[]{:S(2)}, u32[]{:S(2)}) async-start(bf16[128,16,4,128]{3,1,2,0:T(8,128)(2,1)} %bitcast.52), calls=%async_computation.2 | async-start | bytes 4194304 | tf_op jit(solution)/shard_map/all_to_all | solution.py:165
